TPU v7x, 256 devices: a whole 4x4x8 slice. The times are simulated.
256 devices in a mesh: tm: 32 (over x_lo, z, core), rows: 8 (over y, x_hi).
Axes of the slice: x: 4 (x_hi: 2, x_lo: 2; x = x_hi * 2 + x_lo), y: 4, z: 8, core: 2. Of those that a mesh axis runs over, the one named last changes fastest.
Arguments:
- video: bfloat16 [64, 16, 64, 384], P('tm', 'rows'), may hold values from -6 to 6
- conv_weight: bfloat16 [3, 3, 3, 384, 384], replicated, may hold values from -0.0625 to 0.0625
- norm_gain: float32 [384], replicated, may hold values from 0.1 to 1.9
- w_query: bfloat16 [384, 384], replicated, may hold values from -0.3125 to 0.3125
- w_key: bfloat16 [384, 384], replicated, may hold values from -0.875 to 0.875
- w_value: bfloat16 [384, 384], replicated, may hold values from -0.875 to 0.875
- w_out: bfloat16 [384, 384], replicated, may hold values from -0.3125 to 0.3125
- cotangent: bfloat16 [64, 16, 64, 384], P('tm', 'rows'), may hold values from -6 to 6
Outputs:
- block_out: bfloat16 [64, 16, 64, 384], P('tm', 'rows')
- video_grad: bfloat16 [64, 16, 64, 384], P('tm', 'rows')
All inputs are finite; a program needn't handle non-finite values.
Results may differ from a plain program's by a relative error of at most 0.014.
Values may be sent and summed in bfloat16 or wider, within the bound.
No kernel may reach another device: no remote copies, remote signals or barrier semaphores. Data moves between devices by JAX's collectives and lax.ppermute only.
A program may use at most 64 MiB of HBM per device.

v0:
```python
import jax
import jax.numpy as jnp
from jax import lax
from jax.sharding import PartitionSpec as P


def padded_2(cells, sides, width):
    for axis, dim in sides:
        count = lax.axis_size(axis)
        ends = count - 1
        head = lax.slice_in_dim(cells, 0, width, axis=dim)
        tail = lax.slice_in_dim(cells, cells.shape[dim] - width, cells.shape[dim], axis=dim)
        cells = jnp.concatenate(
            [
                lax.ppermute(tail, axis, [(i, (i + 1) % count) for i in range(ends)]),
                cells,
                lax.ppermute(head, axis, [((i + 1) % count, i) for i in range(ends)]),
            ],
            axis=dim,
        )
    return cells


def from_behind(value, axis, by):
    devices = lax.axis_size(axis)
    pairs = [(i, i + by) for i in range(devices) if 0 <= i + by < devices]
    return lax.ppermute(value, axis, pairs)


def convolve(padded, kernel, pads):
    result = lax.conv_general_dilated(
        padded[None],
        kernel,
        (1, 1, 1),
        pads,
        dimension_numbers=("NDHWC", "DHWIO", "NDHWC"),
        preferred_element_type=jnp.float32,
    )
    return result[0]


def project(source, weight):
    return jnp.dot(source.reshape(-1, source.shape[-1]), weight, preferred_element_type=jnp.float32)


def local(video, conv_weight, norm_gain, w_query, w_key, w_value, w_out, cotangent):
    frames, height, width, chans = video.shape
    scale = 1.0 / jnp.sqrt(jnp.float32(chans))
    rimmed = padded_2(video, (("rows", 1),), 1)
    cached = from_behind(rimmed, "tm", 1)
    extended = jnp.concatenate([cached, rimmed], axis=0)
    conv = convolve(extended, conv_weight, [(0, 0), (0, 0), (1, 1)]).astype(jnp.bfloat16)
    convf = conv.astype(jnp.float32)
    inverse = lax.rsqrt(jnp.mean(convf * convf, axis=-1, keepdims=True) + 1e-06)
    normed = convf * inverse * norm_gain
    act = jax.nn.silu(normed).astype(jnp.bfloat16)
    shape4 = (frames, height, width, chans)
    queries = project(act, w_query).astype(jnp.bfloat16).reshape(shape4)
    keys = project(act, w_key).astype(jnp.bfloat16).reshape(shape4)
    values = project(act, w_value).astype(jnp.bfloat16).reshape(shape4)
    keys_all, values_all = (
        lax.all_gather(keys, "rows", axis=1, tiled=True),
        lax.all_gather(values, "rows", axis=1, tiled=True),
    )
    query_flat = queries.reshape(frames, -1, chans)
    keys_flat = keys_all.reshape(frames, -1, chans)
    values_flat = values_all.reshape(frames, -1, chans)
    scores = (
        jnp.einsum("fqc,fkc->fqk", query_flat, keys_flat, preferred_element_type=jnp.float32)
        * scale
    )
    top = jnp.max(scores, axis=-1, keepdims=True)
    expo = jnp.exp(scores - top)
    total = jnp.sum(expo, axis=-1, keepdims=True)
    probs = expo / total
    logsum = (top + jnp.log(total))[:, :, 0]
    attended = jnp.einsum(
        "fqk,fkc->fqc", probs.astype(jnp.bfloat16), values_flat, preferred_element_type=jnp.float32
    ).astype(jnp.bfloat16)
    projected = project(attended, w_out)
    block_out = (
        (act.astype(jnp.float32).reshape(-1, chans) + projected)
        .astype(jnp.bfloat16)
        .reshape(shape4)
    )
    grad_att = project(cotangent, w_out.T).astype(jnp.bfloat16).reshape(frames, -1, chans)
    delta = jnp.sum(grad_att.astype(jnp.float32) * attended.astype(jnp.float32), axis=-1)
    probs_again = jnp.exp(scores - logsum[:, :, None])
    dprob = jnp.einsum("fqc,fkc->fqk", grad_att, values_flat, preferred_element_type=jnp.float32)
    dscore = (probs_again * (dprob - delta[:, :, None])).astype(jnp.bfloat16)
    grad_q = (
        jnp.einsum("fqk,fkc->fqc", dscore, keys_flat, preferred_element_type=jnp.float32) * scale
    ).astype(jnp.bfloat16)
    key_terms = jnp.einsum("fqk,fqc->fkc", dscore, query_flat, preferred_element_type=jnp.float32)
    value_terms = jnp.einsum(
        "fqk,fqc->fkc",
        probs_again.astype(jnp.bfloat16),
        grad_att,
        preferred_element_type=jnp.float32,
    )
    full_shape = (frames, keys_all.shape[1], width, chans)
    key_sum, value_sum = (
        lax.psum_scatter(
            key_terms.reshape(full_shape).astype(jnp.bfloat16),
            "rows",
            scatter_dimension=1,
            tiled=True,
        ).astype(jnp.float32),
        lax.psum_scatter(
            value_terms.reshape(full_shape).astype(jnp.bfloat16),
            "rows",
            scatter_dimension=1,
            tiled=True,
        ).astype(jnp.float32),
    )
    grad_k = (key_sum * scale).astype(jnp.bfloat16).reshape(frames, -1, chans)
    grad_v = value_sum.astype(jnp.bfloat16).reshape(frames, -1, chans)
    grad_act = cotangent.astype(jnp.float32).reshape(-1, chans)
    grad_act = grad_act + project(grad_q, w_query.T)
    grad_act = grad_act + project(grad_k, w_key.T)
    grad_act = grad_act + project(grad_v, w_value.T)
    grad_act = grad_act.reshape(shape4)
    sigma = jax.nn.sigmoid(normed)
    grad_normed = grad_act * sigma * (1.0 + normed * (1.0 - sigma))
    scaled = grad_normed * norm_gain
    grad_conv = inverse * (
        scaled - convf * inverse * inverse * jnp.mean(scaled * convf, axis=-1, keepdims=True)
    )
    grad_conv = grad_conv.astype(jnp.bfloat16)
    flipped = jnp.transpose(jnp.flip(conv_weight, (0, 1, 2)), (0, 1, 2, 4, 3))
    grad_padded = convolve(grad_conv, flipped, [(2, 2), (2, 2), (1, 1)])
    returned = from_behind(grad_padded[:2].astype(jnp.bfloat16), "tm", -1).astype(jnp.float32)
    grad_rimmed = grad_padded[2:]
    grad_rimmed = grad_rimmed.at[frames - 2 :].add(returned)
    from_below = from_behind(grad_rimmed[:, 0].astype(jnp.bfloat16), "rows", -1).astype(jnp.float32)
    from_above = from_behind(grad_rimmed[:, height + 1].astype(jnp.bfloat16), "rows", 1).astype(
        jnp.float32
    )
    inner = grad_rimmed[:, 1 : height + 1]
    inner = inner.at[:, height - 1].add(from_below)
    inner = inner.at[:, 0].add(from_above)
    video_grad = inner.astype(jnp.bfloat16)
    return (block_out, video_grad)


def solution(mesh):
    return jax.shard_map(
        local,
        mesh=mesh,
        in_specs=(
            P("tm", "rows", None, None),
            P(),
            P(),
            P(),
            P(),
            P(),
            P(),
            P("tm", "rows", None, None),
        ),
        out_specs=(P("tm", "rows", None, None), P("tm", "rows", None, None)),
        check_vma=False,
    )
```

profile of v0, /device:TPU:6, one launch (start us, length us, event | category | flops | bytes accessed | tf_op | source)
XLA Modules:
  0.0 364.8 jit_solution(16788286377289315291)
XLA Ops:
  7.2 1.1 fusion.51
  8.4 4.6 %collective-permute-start = (bf16[2,1,64,384]{3,2,1,0:T(8,128)(2,1)S(1)}, bf16[2,1,64,384]{3,2,1,0:T(8,128)(2,1)S(1)}, u32[]{:S(2)}, u32[]{:S(2)}) collective-permute-start(bf16[2,1,64,384]{3,2,1,0:T(8,128)(2,1)S(1)} %get-tuple-element.63), channel_id=1, source_target_pairs={{0,1},{1,2},{2,3},{3,4},{4,5},{5,6},{6,7},{8,9},{9,10},{10,11},{11... | collective-permute-start | bytes 294920 | tf_op jit(solution)/shard_map/ppermute | solution.py:15
  13.0 3.0 collective-permute-start.1
  16.0 0.7 collective-permute-done
  16.6 1.0 constant_dynamic-update-slice_fusion.1
  17.6 4.3 %collective-permute-done.1 = bf16[2,1,64,384]{3,2,1,0:T(8,128)(2,1)S(1)} collective-permute-done((bf16[2,1,64,384]{3,2,1,0:T(8,128)(2,1)S(1)}, bf16[2,1,64,384]{3,2,1,0:T(8,128)(2,1)S(1)}, u32[]{:S(2)}, u32[]{:S(2)}) %collective-permute-start.1) | collective-permute-done | bytes 98336 | tf_op jit(solution)/shard_map/ppermute | solution.py:17
  21.9 1.9 collective-permute-start.2
  23.8 9.3 %collective-permute-done.2 = bf16[2,4,64,384]{3,2,1,0:T(8,128)(2,1)S(1)} collective-permute-done((bf16[2,4,64,384]{3,2,1,0:T(8,128)(2,1)S(1)}, bf16[2,4,64,384]{3,2,1,0:T(8,128)(2,1)S(1)}, u32[]{:S(2)}, u32[]{:S(2)}) %collective-permute-start.2) | collective-permute-done | bytes 393248 | tf_op jit(solution)/shard_map/ppermute | solution.py:27
  34.5 3.4 convert_multiply_fusion.2
  39.1 0.9 convolution_convert_fusion.5
  40.2 0.9 convolution_convert_fusion.4
  42.0 52.6 %all-gather.3.cloned.1.call-done = bf16[2,16,64,384]{3,2,1,0:T(8,128)(2,1)} async-done(((bf16[2,2,64,384]{3,2,1,0:T(8,128)(2,1)}), bf16[2,16,64,384]{3,2,1,0:T(8,128)(2,1)}) %all-gather.3.cloned.1.call-update) | async-done | bytes 1572880 | tf_op jit(solution)/shard_map/all_gather | solution.py:62
  94.5 2.1 fusion.52
  97.0 54.0 %all-gather.5.cloned.1.call-done = bf16[2,16,64,384]{3,2,1,0:T(8,128)(2,1)} async-done(((bf16[2,2,64,384]{3,2,1,0:T(8,128)(2,1)}), bf16[2,16,64,384]{3,2,1,0:T(8,128)(2,1)}) %all-gather.5.cloned.1.call-update) | async-done | bytes 1572880 | tf_op jit(solution)/shard_map/all_gather | solution.py:63
  151.0 2.6 multiply_reduce_fusion
  153.6 1.8 convolution_convert_fusion
  155.4 0.7 fusion.2
  156.1 1.8 convolution_convert_fusion.1
  157.9 0.6 copy-done.14
  161.3 146.1 %all-reduce.5.cloned.1.call-done = (bf16[2,16,64,384]{3,2,1,0:T(8,128)(2,1)}, bf16[2,16,64,384]{3,2,1,0:T(8,128)(2,1)}) async-done(((bf16[2,16,64,384]{3,2,1,0:T(8,128)(2,1)}, bf16[2,16,64,384]{3,2,1,0:T(8,128)(2,1)}), (bf16[2,16,64,384]{3,2,1,0:T(8,128)(2,1)}, bf16[2,16,64,384]{3,2,1,0:T(8,128)(2,1)})) %all-reduce.5.cloned.1.call-update) | async-done | bytes 3145744
  307.4 1.0 multiply_convert_fusion.1
  308.3 1.0 constant_dynamic-slice_fusion
  310.9 17.9 %convolution_select_fusion = f32[4,4,8,9,384]{4,2,3,1,0:T(8,128)S(1)} fusion(bf16[3,3,3,384,384]{4,3,2,1,0:T(8,128)(2,1)} %param.17, pred[8,9]{0,1:T(8,128)(4,1)S(1)} %copy-done.13, bf16[2,2,1,7,2,384]{5,3,4,1,0,2:T(8,128)(2,1)S(1)} %slice.130, bf16[2,2,1,8,9,384]{5,3,4,1,0,2:T(8,128)(2,1)S(1)} %copy.100), kind=kOutput, calls=%fused_computation.4 | convolution fusion | flops 2294489088 | bytes 9996360 | tf_op jit(solution)/shard_map/conv_general_dilated | solution.py:31
  329.2 3.9 %collective-permute-start.3 = (bf16[2,4,64,384]{3,1,2,0:T(4,128)(2,1)S(1)}, bf16[2,4,64,384]{3,1,2,0:T(4,128)(2,1)S(1)}, u32[]{:S(2)}, u32[]{:S(2)}) collective-permute-start(bf16[2,4,64,384]{3,1,2,0:T(4,128)(2,1)S(1)} %slice_bitcast_fusion.1), channel_id=1, source_target_pairs={{8,0},{16,8},{24,16},{32,24},{40,32},{48,40},{56,48},{64,56},{72,6... | collective-permute-start | bytes 1179656 | tf_op jit(solution)/shard_map/ppermute | solution.py:27
  333.4 5.0 %collective-permute-done.3 = bf16[2,4,64,384]{3,1,2,0:T(4,128)(2,1)S(1)} collective-permute-done((bf16[2,4,64,384]{3,1,2,0:T(4,128)(2,1)S(1)}, bf16[2,4,64,384]{3,1,2,0:T(4,128)(2,1)S(1)}, u32[]{:S(2)}, u32[]{:S(2)}) %collective-permute-start.3) | collective-permute-done | bytes 393248 | tf_op jit(solution)/shard_map/ppermute | solution.py:27
  339.0 5.7 %collective-permute-start.4 = (bf16[2,64,384]{2,1,0:T(8,128)(2,1)S(1)}, bf16[2,64,384]{2,1,0:T(8,128)(2,1)S(1)}, u32[]{:S(2)}, u32[]{:S(2)}) collective-permute-start(bf16[2,64,384]{2,1,0:T(8,128)(2,1)S(1)} %bitcast.126), channel_id=1, source_target_pairs={{1,0},{2,1},{3,2},{4,3},{5,4},{6,5},{7,6},{9,8},{10,9},{11,10},{12... | collective-permute-start | bytes 294920 | tf_op jit(solution)/shard_map/ppermute | solution.py:27
  344.7 0.9 fusion.5
  345.9 2.5 collective-permute-start.5
  348.8 3.2 scatter-add.6
  352.0 1.9 collective-permute-done.5
  354.1 3.2 scatter-add.9
  357.5 0.7 copy.103
  (85 shorter events, 9.5 us)
Async XLA Ops:
  7.2 33.0 %copy-start = (bf16[384,384]{1,0:T(8,128)(2,1)S(1)}, bf16[384,384]{1,0:T(8,128)(2,1)}, u32[]{:S(2)}) copy-start(bf16[384,384]{1,0:T(8,128)(2,1)} %param.21) | copy-start | bytes 884740
  7.2 87.4 %all-gather.3.cloned.1.call-start = ((), (), s32[]{:S(2)}) async-start(), calls=%async_computation | async-start | bytes 1769472 | tf_op jit(solution)/shard_map/all_gather | solution.py:62
  7.2 27.1 %copy-start.1 = (bf16[3,3,3,384,384]{4,3,2,1,0:T(8,128)(2,1)S(1)}, bf16[3,3,3,384,384]{4,3,2,1,0:T(8,128)(2,1)}, u32[]{:S(2)}) copy-start(bf16[3,3,3,384,384]{4,3,2,1,0:T(8,128)(2,1)} %param.17) | copy-start | bytes 23887876
  8.4 8.3 %collective-permute-start = (bf16[2,1,64,384]{3,2,1,0:T(8,128)(2,1)S(1)}, bf16[2,1,64,384]{3,2,1,0:T(8,128)(2,1)S(1)}, u32[]{:S(2)}, u32[]{:S(2)}) collective-permute-start(bf16[2,1,64,384]{3,2,1,0:T(8,128)(2,1)S(1)} %get-tuple-element.63), channel_id=1, source_target_pairs={{0,1},{1,2},{2,3},{3,4},{4,5},{5,6},{6,7},{8,9},{9,10},{10,11},{11... | collective-permute-start | bytes 294920 | tf_op jit(solution)/shard_map/ppermute | solution.py:15
  13.0 8.9 %collective-permute-start.1 = (bf16[2,1,64,384]{3,2,1,0:T(8,128)(2,1)S(1)}, bf16[2,1,64,384]{3,2,1,0:T(8,128)(2,1)S(1)}, u32[]{:S(2)}, u32[]{:S(2)}) collective-permute-start(bf16[2,1,64,384]{3,2,1,0:T(8,128)(2,1)S(1)} %get-tuple-element.62), channel_id=1, source_target_pairs={{1,0},{2,1},{3,2},{4,3},{5,4},{6,5},{7,6},{9,8},{10,9},{11,10},{12... | collective-permute-start | bytes 294920 | tf_op jit(solution)/shard_map/ppermute | solution.py:17
  21.9 11.2 %collective-permute-start.2 = (bf16[2,4,64,384]{3,2,1,0:T(8,128)(2,1)S(1)}, bf16[2,4,64,384]{3,2,1,0:T(8,128)(2,1)S(1)}, u32[]{:S(2)}, u32[]{:S(2)}) collective-permute-start(bf16[2,4,64,384]{3,2,1,0:T(8,128)(2,1)S(1)} %constant_dynamic-update-slice_fusion), channel_id=1, source_target_pairs={{0,8},{8,16},{16,24},{24,32},{32,40},{40,48},{48,56},{56,64},{64,7... | collective-permute-start | bytes 1179656 | tf_op jit(solution)/shard_map/ppermute | solution.py:27
  33.8 0.7 copy-start.13
  37.9 1.1 copy-start.12
  37.9 1.2 copy-start.4
  38.5 2.9 copy-start.5
  38.5 2.9 copy-start.9
  38.7 3.0 copy-start.7
  40.1 110.9 %all-gather.5.cloned.1.call-start = ((), (), s32[]{:S(2)}) async-start(), calls=%async_computation.1 | async-start | bytes 1769472 | tf_op jit(solution)/shard_map/all_gather | solution.py:63
  41.1 266.2 %all-reduce.5.cloned.1.call-start = ((), (), s32[]{:S(2)}) async-start(), calls=%async_computation.2 | async-start | bytes 6291456
  153.6 1.8 copy-start.3
  157.9 0.7 copy-start.14
  157.9 2.2 copy-start.2
  159.9 1.0 copy-start.8
  160.0 1.0 copy-start.10
  329.2 9.2 %collective-permute-start.3 = (bf16[2,4,64,384]{3,1,2,0:T(4,128)(2,1)S(1)}, bf16[2,4,64,384]{3,1,2,0:T(4,128)(2,1)S(1)}, u32[]{:S(2)}, u32[]{:S(2)}) collective-permute-start(bf16[2,4,64,384]{3,1,2,0:T(4,128)(2,1)S(1)} %slice_bitcast_fusion.1), channel_id=1, source_target_pairs={{8,0},{16,8},{24,16},{32,24},{40,32},{48,40},{56,48},{64,56},{72,6... | collective-permute-start | bytes 1179656 | tf_op jit(solution)/shard_map/ppermute | solution.py:27
  338.4 6.3 %copy-start.6 = (bf16[384,384]{1,0:T(8,128)(2,1)S(1)}, bf16[384,384]{1,0:T(8,128)(2,1)}, u32[]{:S(2)}) copy-start(bf16[384,384]{1,0:T(8,128)(2,1)} %param.22) | copy-start | bytes 884740
  338.4 6.3 %copy-start.11 = (bf16[2,128,384]{2,1,0:T(8,128)(2,1)S(1)}, bf16[2,128,384]{2,1,0:T(8,128)(2,1)}, u32[]{:S(2)}) copy-start(bf16[2,128,384]{2,1,0:T(8,128)(2,1)} %get-tuple-element.69) | copy-start | bytes 589828
  339.0 9.5 %collective-permute-start.4 = (bf16[2,64,384]{2,1,0:T(8,128)(2,1)S(1)}, bf16[2,64,384]{2,1,0:T(8,128)(2,1)S(1)}, u32[]{:S(2)}, u32[]{:S(2)}) collective-permute-start(bf16[2,64,384]{2,1,0:T(8,128)(2,1)S(1)} %bitcast.126), channel_id=1, source_target_pairs={{1,0},{2,1},{3,2},{4,3},{5,4},{6,5},{7,6},{9,8},{10,9},{11,10},{12... | collective-permute-start | bytes 294920 | tf_op jit(solution)/shard_map/ppermute | solution.py:27
  345.9 8.0 %collective-permute-start.5 = (bf16[2,64,384]{2,1,0:T(8,128)(2,1)S(1)}, bf16[2,64,384]{2,1,0:T(8,128)(2,1)S(1)}, u32[]{:S(2)}, u32[]{:S(2)}) collective-permute-start(bf16[2,64,384]{2,1,0:T(8,128)(2,1)S(1)} %bitcast.127), channel_id=1, source_target_pairs={{0,1},{1,2},{2,3},{3,4},{4,5},{5,6},{6,7},{8,9},{9,10},{10,11},{11... | collective-permute-start | bytes 294920 | tf_op jit(solution)/shard_map/ppermute | solution.py:27
Sparse Core Ops, SparseCore 0:
  40.2 54.2 all-gather.2
  97.7 53.2 all-gather.4
  158.0 149.3 all-reduce.4
where the time goes:
time: 365 us
  waiting for transfers between devices  274 us (75%)
  matrix products  35.1 us (10%)
  starting transfers between devices  22 us (6%)
  local copies, waits for them, and re-layouts  15.9 us (4%)
  between operations  15 us (4%)
    unnamed x4, waiting for transfers between devices  146 us
    all_gather x1, waiting for transfers between devices, local(): lax.all_gather(values, 'rows', axis=1, tiled=True)  54 us
    all_gather x1, waiting for transfers between devices, local(): lax.all_gather(keys, 'rows', axis=1, tiled=True)  52.6 us
    conv_general_dilated x2, matrix products, convolve(): lax.conv_general_dilated(padded[None], kernel, (1, 1, 1), pads, dimension...  21.3 us
    ppermute x4, waiting for transfers between devices, from_behind(): return lax.ppermute(value, axis, pairs)  16.1 us
    ppermute x4, starting transfers between devices, from_behind(): return lax.ppermute(value, axis, pairs)  14.1 us
  transfers between devices with their start and end apart: 9, of which 8 were waited for; matrix products, arithmetic and copies ran while one was open for 3% of the time, Pallas kernels for 0%

commit v1 on v0

--- a/solution.py
+++ b/solution.py
@@ -2,6 +2,11 @@
 import jax.numpy as jnp
 from jax import lax
 from jax.sharding import PartitionSpec as P
+
+
+def all_by_exchange(block, axis, dim):
+    stack = jnp.stack([block] * lax.axis_size(axis))
+    return jnp.concatenate(lax.all_to_all(stack, axis, 0, 0), axis=dim)
 
 
 def padded_2(cells, sides, width):
@@ -60,7 +65,7 @@
     values = project(act, w_value).astype(jnp.bfloat16).reshape(shape4)
     keys_all, values_all = (
         lax.all_gather(keys, "rows", axis=1, tiled=True),
-        lax.all_gather(values, "rows", axis=1, tiled=True),
+        all_by_exchange(values, "rows", 1),
     )
     query_flat = queries.reshape(frames, -1, chans)
     keys_flat = keys_all.reshape(frames, -1, chans)

time: 365 us -> 316 us (0.87)
  waiting for transfers between devices: 274 us -> 216 us
  starting transfers between devices: 22 us -> 29 us
    all_gather x1 -> x0, waiting for transfers between devices: 54 us -> none  [local(): lax.all_gather(values, 'rows', axis=1, tiled=True)]
    all_gather x1, waiting for transfers between devices: 52.6 us -> 30.3 us  [local(): lax.all_gather(keys, 'rows', axis=1, tiled=True)]
    all_to_all x0 -> x1, waiting for transfers between devices: none -> 18.7 us  [all_by_exchange(): return jnp.concatenate(lax.all_to_all(stack, axis, 0, 0), axis=dim)]
    all_to_all x0 -> x1, starting transfers between devices: none -> 7.28 us  [all_by_exchange(): return jnp.concatenate(lax.all_to_all(stack, axis, 0, 0), axis=dim)]
    unnamed x4 -> x3, waiting for transfers between devices: 146 us -> 146 us
  transfers between devices with their start and end apart: 9 -> 9, of which waited for: 8 -> 8; matrix products, arithmetic and copies ran while one was open for 3% -> 4% of each run, Pallas kernels for 0% -> 0%
where the time goes in v1:
time: 316 us
  waiting for transfers between devices  216 us (68%)
  matrix products  34 us (11%)
  starting transfers between devices  29 us (9%)
  local copies, waits for them, and re-layouts  18.1 us (6%)
  between operations  15.3 us (5%)
    unnamed x3, waiting for transfers between devices  146 us
    all_gather x1, waiting for transfers between devices, local(): lax.all_gather(keys, 'rows', axis=1, tiled=True)  30.3 us
    conv_general_dilated x2, matrix products, convolve(): lax.conv_general_dilated(padded[None], kernel, (1, 1, 1), pads, dimension...  21.3 us
    all_to_all x1, waiting for transfers between devices, all_by_exchange(): return jnp.concatenate(lax.all_to_all(stack, axis, 0, 0), axis=dim)  18.7 us
    ppermute x4, waiting for transfers between devices, from_behind(): return lax.ppermute(value, axis, pairs)  16.1 us
    ppermute x4, starting transfers between devices, from_behind(): return lax.ppermute(value, axis, pairs)  14.1 us
    all_to_all x1, starting transfers between devices, all_by_exchange(): return jnp.concatenate(lax.all_to_all(stack, axis, 0, 0), axis=dim)  7.28 us
  transfers between devices with their start and end apart: 9, of which 8 were waited for; matrix products, arithmetic and copies ran while one was open for 4% of the time, Pallas kernels for 0%

profile of v1, /device:TPU:6, one launch (start us, length us, event | category | flops | bytes accessed | tf_op | source)
XLA Modules:
  0.0 315.6 jit_solution(6890522990548540437)
XLA Ops:
  7.2 1.1 fusion.51
  8.4 4.6 %collective-permute-start = (bf16[2,1,64,384]{3,2,1,0:T(8,128)(2,1)S(1)}, bf16[2,1,64,384]{3,2,1,0:T(8,128)(2,1)S(1)}, u32[]{:S(2)}, u32[]{:S(2)}) collective-permute-start(bf16[2,1,64,384]{3,2,1,0:T(8,128)(2,1)S(1)} %get-tuple-element.63), channel_id=1, source_target_pairs={{0,1},{1,2},{2,3},{3,4},{4,5},{5,6},{6,7},{8,9},{9,10},{10,11},{11... | collective-permute-start | bytes 294920 | tf_op jit(solution)/shard_map/ppermute | solution.py:20
  13.0 3.0 collective-permute-start.1
  16.6 1.0 constant_dynamic-update-slice_fusion.1
  17.6 4.3 %collective-permute-done.1 = bf16[2,1,64,384]{3,2,1,0:T(8,128)(2,1)S(1)} collective-permute-done((bf16[2,1,64,384]{3,2,1,0:T(8,128)(2,1)S(1)}, bf16[2,1,64,384]{3,2,1,0:T(8,128)(2,1)S(1)}, u32[]{:S(2)}, u32[]{:S(2)}) %collective-permute-start.1) | collective-permute-done | bytes 98336 | tf_op jit(solution)/shard_map/ppermute | solution.py:22
  21.9 1.9 collective-permute-start.2
  23.8 9.3 %collective-permute-done.2 = bf16[2,4,64,384]{3,2,1,0:T(8,128)(2,1)S(1)} collective-permute-done((bf16[2,4,64,384]{3,2,1,0:T(8,128)(2,1)S(1)}, bf16[2,4,64,384]{3,2,1,0:T(8,128)(2,1)S(1)}, u32[]{:S(2)}, u32[]{:S(2)}) %collective-permute-start.2) | collective-permute-done | bytes 393248 | tf_op jit(solution)/shard_map/ppermute | solution.py:32
  34.5 3.4 %convert_multiply_fusion.2 = (f32[2,2,8,9,384]{4,2,3,1,0:T(8,128)S(1)}, bf16[2,2,8,9,384]{4,2,3,1,0:T(8,128)(2,1)S(1)}) fusion(bf16[3,3,3,384,384]{4,3,2,1,0:T(8,128)(2,1)S(1)} %copy-done.1, bf16[4,4,1,7,2,384]{5,3,4,1,0,2:T(8,128)(2,1)S(1)} %slice.126, bf16[4,4,1,8,9,384]{5,3,4,1,0,2:T(8,128)(2,1)S(1)} %copy.90, pred[8,9]{0,1:T(8,128)(4,1)S(1)} %copy-done.20), kind=kOutput, calls=%fused_computation.73 | convolution fusion | flops 2296922112 | bytes 9683016 | tf_op jit(solution)/shard_map/conv_general_dilated | solution.py:36
  39.4 0.9 convolution_convert_fusion.5
  40.7 1.4 stack.3
  42.1 7.3 %all-to-all-start = ((bf16[8,2,2,64,384]{4,3,2,1,0:T(8,128)(2,1)}), bf16[8,2,2,64,384]{4,3,2,1,0:T(8,128)(2,1)S(1)}, u32[]{:S(2)}, u32[]{:S(2)}) async-start(bf16[8,2,2,64,384]{4,3,2,1,0:T(8,128)(2,1)} %stack.3), calls=%async_computation | async-start | bytes 3145728 | tf_op jit(solution)/shard_map/all_to_all | solution.py:9
  49.4 1.0 convolution_convert_fusion.3
  50.4 0.9 convolution_convert_fusion.6
  51.3 18.7 %all-to-all-done = bf16[8,2,2,64,384]{4,3,2,1,0:T(8,128)(2,1)S(1)} async-done(((bf16[8,2,2,64,384]{4,3,2,1,0:T(8,128)(2,1)}), bf16[8,2,2,64,384]{4,3,2,1,0:T(8,128)(2,1)S(1)}, u32[]{:S(2)}, u32[]{:S(2)}) %all-to-all-start) | async-done | bytes 1572896 | tf_op jit(solution)/shard_map/all_to_all | solution.py:9
  70.2 30.3 %all-gather.2.cloned.1.call-done = bf16[2,16,64,384]{3,2,1,0:T(8,128)(2,1)} async-done(((bf16[2,2,64,384]{3,2,1,0:T(8,128)(2,1)}), bf16[2,16,64,384]{3,2,1,0:T(8,128)(2,1)}) %all-gather.2.cloned.1.call-update) | async-done | bytes 1572880 | tf_op jit(solution)/shard_map/all_gather | solution.py:67
  100.6 2.3 fusion.52
  103.8 1.9 convolution_convert_fusion
  105.6 0.7 fusion.2
  106.6 1.8 convolution_convert_fusion.1
  111.8 146.1 %all-reduce.5.cloned.1.call-done = (bf16[2,16,64,384]{3,2,1,0:T(8,128)(2,1)}, bf16[2,16,64,384]{3,2,1,0:T(8,128)(2,1)}) async-done(((bf16[2,16,64,384]{3,2,1,0:T(8,128)(2,1)}, bf16[2,16,64,384]{3,2,1,0:T(8,128)(2,1)}), (bf16[2,16,64,384]{3,2,1,0:T(8,128)(2,1)}, bf16[2,16,64,384]{3,2,1,0:T(8,128)(2,1)})) %all-reduce.5.cloned.1.call-update) | async-done | bytes 3145744
  257.9 1.0 multiply_convert_fusion.1
  258.9 1.0 constant_dynamic-slice_fusion
  261.5 17.9 %convolution_select_fusion = f32[4,4,8,9,384]{4,2,3,1,0:T(8,128)S(1)} fusion(bf16[3,3,3,384,384]{4,3,2,1,0:T(8,128)(2,1)} %param.17, pred[8,9]{0,1:T(8,128)(4,1)S(1)} %copy-done.20, bf16[2,2,1,7,2,384]{5,3,4,1,0,2:T(8,128)(2,1)S(1)} %slice.130, bf16[2,2,1,8,9,384]{5,3,4,1,0,2:T(8,128)(2,1)S(1)} %copy.102), kind=kOutput, calls=%fused_computation.4 | convolution fusion | flops 2294489088 | bytes 9996360 | tf_op jit(solution)/shard_map/conv_general_dilated | solution.py:36
  279.8 3.9 %collective-permute-start.3 = (bf16[2,4,64,384]{3,1,2,0:T(4,128)(2,1)S(1)}, bf16[2,4,64,384]{3,1,2,0:T(4,128)(2,1)S(1)}, u32[]{:S(2)}, u32[]{:S(2)}) collective-permute-start(bf16[2,4,64,384]{3,1,2,0:T(4,128)(2,1)S(1)} %slice_bitcast_fusion.1), channel_id=1, source_target_pairs={{8,0},{16,8},{24,16},{32,24},{40,32},{48,40},{56,48},{64,56},{72,6... | collective-permute-start | bytes 1179656 | tf_op jit(solution)/shard_map/ppermute | solution.py:32
  284.0 5.0 %collective-permute-done.3 = bf16[2,4,64,384]{3,1,2,0:T(4,128)(2,1)S(1)} collective-permute-done((bf16[2,4,64,384]{3,1,2,0:T(4,128)(2,1)S(1)}, bf16[2,4,64,384]{3,1,2,0:T(4,128)(2,1)S(1)}, u32[]{:S(2)}, u32[]{:S(2)}) %collective-permute-start.3) | collective-permute-done | bytes 393248 | tf_op jit(solution)/shard_map/ppermute | solution.py:32
  289.5 5.7 %collective-permute-start.4 = (bf16[2,64,384]{2,1,0:T(8,128)(2,1)S(1)}, bf16[2,64,384]{2,1,0:T(8,128)(2,1)S(1)}, u32[]{:S(2)}, u32[]{:S(2)}) collective-permute-start(bf16[2,64,384]{2,1,0:T(8,128)(2,1)S(1)} %bitcast.128), channel_id=1, source_target_pairs={{1,0},{2,1},{3,2},{4,3},{5,4},{6,5},{7,6},{9,8},{10,9},{11,10},{12... | collective-permute-start | bytes 294920 | tf_op jit(solution)/shard_map/ppermute | solution.py:32
  295.3 0.9 fusion.5
  296.5 2.5 collective-permute-start.5
  299.4 3.2 %scatter-add.6 = f32[2,2,64,384]{3,1,2,0:T(2,128)S(1)} dynamic-update-slice(f32[2,2,64,384]{3,1,2,0:T(2,128)S(1)} %slice.135, f32[2,1,64,384]{3,1,2,0:T(1,128)S(1)} %slice_add_fusion.1, s32[]{:T(128)} %constant.106.clone.1, s32[]{:T(128)} %constant.107.clone.1, s32[]{:T(128)} %constant.106.clone.1, s32[]{:T(128)} %constant.106.clone.1) | dynamic-update-slice | bytes 393220 | tf_op jit(solution)/shard_map/scatter-add | solution.py:145
  302.6 1.9 collective-permute-done.5
  304.7 3.2 %scatter-add.9 = f32[2,2,64,384]{3,1,2,0:T(2,128)S(1)} dynamic-update-slice(f32[2,2,64,384]{3,1,2,0:T(2,128)S(1)} %scatter-add.6, f32[2,1,64,384]{3,1,2,0:T(1,128)S(1)} %slice_add_fusion, s32[]{:T(128)} %constant.106.clone.1, s32[]{:T(128)} %constant.106.clone.1, s32[]{:T(128)} %constant.106.clone.1, s32[]{:T(128)} %constant.106.clone.1) | dynamic-update-slice | bytes 393220 | tf_op jit(solution)/shard_map/scatter-add | solution.py:146
  308.1 0.7 copy.105
  (100 shorter events, 11.7 us)
Async XLA Ops:
  7.2 33.2 %copy-start = (bf16[384,384]{1,0:T(8,128)(2,1)S(1)}, bf16[384,384]{1,0:T(8,128)(2,1)}, u32[]{:S(2)}) copy-start(bf16[384,384]{1,0:T(8,128)(2,1)} %param.21) | copy-start | bytes 884740
  7.2 93.4 %all-gather.2.cloned.1.call-start = ((), (), s32[]{:S(2)}) async-start(), calls=%async_computation.1 | async-start | bytes 1769472 | tf_op jit(solution)/shard_map/all_gather | solution.py:67
  7.2 27.1 %copy-start.1 = (bf16[3,3,3,384,384]{4,3,2,1,0:T(8,128)(2,1)S(1)}, bf16[3,3,3,384,384]{4,3,2,1,0:T(8,128)(2,1)}, u32[]{:S(2)}) copy-start(bf16[3,3,3,384,384]{4,3,2,1,0:T(8,128)(2,1)} %param.17) | copy-start | bytes 23887876
  8.4 8.3 %collective-permute-start = (bf16[2,1,64,384]{3,2,1,0:T(8,128)(2,1)S(1)}, bf16[2,1,64,384]{3,2,1,0:T(8,128)(2,1)S(1)}, u32[]{:S(2)}, u32[]{:S(2)}) collective-permute-start(bf16[2,1,64,384]{3,2,1,0:T(8,128)(2,1)S(1)} %get-tuple-element.63), channel_id=1, source_target_pairs={{0,1},{1,2},{2,3},{3,4},{4,5},{5,6},{6,7},{8,9},{9,10},{10,11},{11... | collective-permute-start | bytes 294920 | tf_op jit(solution)/shard_map/ppermute | solution.py:20
  13.0 8.9 %collective-permute-start.1 = (bf16[2,1,64,384]{3,2,1,0:T(8,128)(2,1)S(1)}, bf16[2,1,64,384]{3,2,1,0:T(8,128)(2,1)S(1)}, u32[]{:S(2)}, u32[]{:S(2)}) collective-permute-start(bf16[2,1,64,384]{3,2,1,0:T(8,128)(2,1)S(1)} %get-tuple-element.62), channel_id=1, source_target_pairs={{1,0},{2,1},{3,2},{4,3},{5,4},{6,5},{7,6},{9,8},{10,9},{11,10},{12... | collective-permute-start | bytes 294920 | tf_op jit(solution)/shard_map/ppermute | solution.py:22
  21.9 11.2 %collective-permute-start.2 = (bf16[2,4,64,384]{3,2,1,0:T(8,128)(2,1)S(1)}, bf16[2,4,64,384]{3,2,1,0:T(8,128)(2,1)S(1)}, u32[]{:S(2)}, u32[]{:S(2)}) collective-permute-start(bf16[2,4,64,384]{3,2,1,0:T(8,128)(2,1)S(1)} %constant_dynamic-update-slice_fusion), channel_id=1, source_target_pairs={{0,8},{8,16},{16,24},{24,32},{32,40},{40,48},{48,56},{56,64},{64,7... | collective-permute-start | bytes 1179656 | tf_op jit(solution)/shard_map/ppermute | solution.py:32
  33.8 0.7 copy-start.20
  37.9 0.7 copy-start.13
  37.9 1.3 copy-start.19
  37.9 1.5 copy-start.7
  38.6 2.1 copy-start.15
  39.4 10.9 %copy-start.3 = (bf16[256,384]{1,0:T(8,128)(2,1)}, bf16[256,384]{1,0:T(8,128)(2,1)S(1)}, u32[]{:S(2)}) copy-start(bf16[256,384]{1,0:T(8,128)(2,1)S(1)} %fusion.28) | copy-start | bytes 589828
  42.1 7.3 %copy-start.9 = (bf16[384,384]{1,0:T(8,128)(2,1)S(1)}, bf16[384,384]{1,0:T(8,128)(2,1)}, u32[]{:S(2)}) copy-start(bf16[384,384]{1,0:T(8,128)(2,1)} %param.22) | copy-start | bytes 884740
  42.1 7.3 %copy-start.17 = (bf16[2,2,64,384]{3,2,1,0:T(8,128)(2,1)S(1)}, bf16[2,2,64,384]{3,2,1,0:T(8,128)(2,1)}, u32[]{:S(2)}) copy-start(bf16[2,2,64,384]{3,2,1,0:T(8,128)(2,1)} %param.23) | copy-start | bytes 589828
  42.1 8.3 %copy-start.11 = (bf16[384,384]{1,0:T(8,128)(2,1)S(1)}, bf16[384,384]{1,0:T(8,128)(2,1)}, u32[]{:S(2)}) copy-start(bf16[384,384]{1,0:T(8,128)(2,1)} %param.19) | copy-start | bytes 884740
  42.1 27.9 %all-to-all-start = ((bf16[8,2,2,64,384]{4,3,2,1,0:T(8,128)(2,1)}), bf16[8,2,2,64,384]{4,3,2,1,0:T(8,128)(2,1)S(1)}, u32[]{:S(2)}, u32[]{:S(2)}) async-start(bf16[8,2,2,64,384]{4,3,2,1,0:T(8,128)(2,1)} %stack.3), calls=%async_computation | async-start | bytes 3145728 | tf_op jit(solution)/shard_map/all_to_all | solution.py:9
  49.4 208.5 %all-reduce.5.cloned.1.call-start = ((), (), s32[]{:S(2)}) async-start(), calls=%async_computation.2 | async-start | bytes 6291456
  100.6 2.6 copy-start.6
  105.6 0.9 copy-start.5
  108.4 0.7 copy-start.21
  108.4 1.9 copy-start.14
  108.4 2.2 copy-start.2
  110.5 1.0 copy-start.12
  110.5 1.0 copy-start.18
  110.6 149.2 %copy-start.8 = (bf16[384,384]{1,0:T(8,128)(2,1)S(1)}, bf16[384,384]{1,0:T(8,128)(2,1)}, u32[]{:S(2)}) copy-start(bf16[384,384]{1,0:T(8,128)(2,1)} %param.20) | copy-start | bytes 884740
  111.5 148.6 %copy-start.16 = (bf16[2,2,1,64,384]{4,3,2,1,0:T(8,128)(2,1)S(1)}, bf16[2,2,1,64,384]{4,3,2,1,0:T(8,128)(2,1)}, u32[]{:S(2)}) copy-start(bf16[2,2,1,64,384]{4,3,2,1,0:T(8,128)(2,1)} %copy-done.15) | copy-start | bytes 589828
  279.8 9.2 %collective-permute-start.3 = (bf16[2,4,64,384]{3,1,2,0:T(4,128)(2,1)S(1)}, bf16[2,4,64,384]{3,1,2,0:T(4,128)(2,1)S(1)}, u32[]{:S(2)}, u32[]{:S(2)}) collective-permute-start(bf16[2,4,64,384]{3,1,2,0:T(4,128)(2,1)S(1)} %slice_bitcast_fusion.1), channel_id=1, source_target_pairs={{8,0},{16,8},{24,16},{32,24},{40,32},{48,40},{56,48},{64,56},{72,6... | collective-permute-start | bytes 1179656 | tf_op jit(solution)/shard_map/ppermute | solution.py:32
  289.0 6.3 %copy-start.4 = (bf16[256,384]{1,0:T(8,128)(2,1)S(1)}, bf16[256,384]{1,0:T(8,128)(2,1)}, u32[]{:S(2)}) copy-start(bf16[256,384]{1,0:T(8,128)(2,1)} %copy-done.3) | copy-start | bytes 589828
  289.0 6.3 %copy-start.10 = (bf16[384,384]{1,0:T(8,128)(2,1)S(1)}, bf16[384,384]{1,0:T(8,128)(2,1)}, u32[]{:S(2)}) copy-start(bf16[384,384]{1,0:T(8,128)(2,1)} %param.22) | copy-start | bytes 884740
  289.5 9.5 %collective-permute-start.4 = (bf16[2,64,384]{2,1,0:T(8,128)(2,1)S(1)}, bf16[2,64,384]{2,1,0:T(8,128)(2,1)S(1)}, u32[]{:S(2)}, u32[]{:S(2)}) collective-permute-start(bf16[2,64,384]{2,1,0:T(8,128)(2,1)S(1)} %bitcast.128), channel_id=1, source_target_pairs={{1,0},{2,1},{3,2},{4,3},{5,4},{6,5},{7,6},{9,8},{10,9},{11,10},{12... | collective-permute-start | bytes 294920 | tf_op jit(solution)/shard_map/ppermute | solution.py:32
  296.5 8.0 %collective-permute-start.5 = (bf16[2,64,384]{2,1,0:T(8,128)(2,1)S(1)}, bf16[2,64,384]{2,1,0:T(8,128)(2,1)S(1)}, u32[]{:S(2)}, u32[]{:S(2)}) collective-permute-start(bf16[2,64,384]{2,1,0:T(8,128)(2,1)S(1)} %bitcast.129), channel_id=1, source_target_pairs={{0,1},{1,2},{2,3},{3,4},{4,5},{5,6},{6,7},{8,9},{9,10},{10,11},{11... | collective-permute-start | bytes 294920 | tf_op jit(solution)/shard_map/ppermute | solution.py:32
Sparse Core Ops, SparseCore 0:
  40.5 60.0 all-gather.1
  108.5 149.3 all-reduce.4
